TPU v7x, 32 devices: a whole 2x2x4 slice. The times are simulated.
32 devices in a mesh: section: 2 (over core), row: 4 (over y, x), col: 4 (over z).
Axes of the slice: x: 2, y: 2, z: 4, core: 2. Of those that a mesh axis runs over, the one named last changes fastest.
Arguments:
- tables: bfloat16 [32, 1024, 256], P('col', ('section', 'row')), may hold values from -1.5 to 1.5
- bag_index: int32 [128, 32, 32], P(None, 'col'), may hold values from 0 to 1024, as said below
- cross_weight: bfloat16 [2, 8192, 8192], P(None, 'col', ('section', 'row')), may hold values from -0.0625 to 0.0625
- cross_bias: float32 [2, 8192], replicated, may hold values from -3 to 3
- upstream: bfloat16 [128, 8192], P(('section', 'row'), 'col'), may hold values from -6 to 6
Outputs:
- crossed: bfloat16 [128, 8192], P(('section', 'row'), 'col')
- pooled_grad: float32 [128, 8192], P(('section', 'row'), 'col')
- table_grad: float32 [32, 1024, 256], P('col', ('section', 'row'))
- weight_grad: float32 [2, 8192, 8192], P(None, 'col', ('section', 'row'))
- bias_grad: float32 [2, 8192], P(None, ('section', 'row'))
Inputs may be any that keep to these rules, and one draw needn't show every extreme that they name: `bag_index`: each bag lists 1 to 32 table rows first, then only the padding value 1024, which stands for a zero row.
All inputs are finite; a program needn't handle non-finite values.
Results may differ from a plain program's by a relative error of at most 0.012.
Values may be sent and summed in bfloat16 or wider, within the bound.
A program may use at most 128 MiB of HBM per device.

v0:
```python
import math

import jax
import jax.numpy as jnp
from jax import lax
from jax.sharding import PartitionSpec as P


def bag_counts(local_ids, shard_rows):
    slot_ids = lax.broadcasted_iota(jnp.int32, (1, 1, shard_rows), 2)
    bag_len = local_ids.shape[1]
    group_size = math.gcd(bag_len, 8)
    summed = jnp.zeros((local_ids.shape[0], shard_rows), jnp.float32)
    for offset in range(0, bag_len, group_size):
        matches = local_ids[:, offset : offset + group_size, None] == slot_ids
        summed = summed + jnp.sum(matches, axis=1, dtype=jnp.float32)
    return summed.astype(jnp.bfloat16)


def body(tables, bag_index, cross_weight, cross_bias, upstream):
    feat_count, shard_rows, entry_width = tables.shape
    batch_rows = bag_index.shape[0]
    layers, in_width, out_width = cross_weight.shape
    block_rows = upstream.shape[0]
    np_count = lax.axis_size(("section", "row"))
    col_count = lax.axis_size("col")
    my_row = lax.axis_index(("section", "row"))
    local_ids = bag_index - my_row * shard_rows
    counts = jnp.stack(
        [bag_counts(local_ids[:, feature_at, :], shard_rows) for feature_at in range(feat_count)]
    )
    pooled_part = jnp.einsum("fbv,fve->bfe", counts, tables, preferred_element_type=jnp.float32)
    pooled = lax.psum_scatter(
        pooled_part.reshape(
            lax.axis_size(("section", "row")) * block_rows, feat_count * entry_width
        ),
        ("section", "row"),
        scatter_dimension=0,
        tiled=True,
    ).astype(jnp.bfloat16)
    pooled_wide = pooled.astype(jnp.float32)
    current = pooled
    kept_inputs = []
    kept_mixed = []
    for layer_at in range(layers):
        gathered = lax.all_gather(current, ("section", "row"), axis=0, tiled=True)
        partial_value = jnp.dot(
            gathered, cross_weight[layer_at], preferred_element_type=jnp.float32
        )
        strip_rows = batch_rows // (np_count * col_count)
        grid_sums = partial_value.reshape(np_count, col_count, strip_rows, out_width)
        summed = lax.psum_scatter(grid_sums, "col", scatter_dimension=1, tiled=True).reshape(
            np_count * strip_rows, out_width
        )
        summed = summed + lax.dynamic_slice_in_dim(
            cross_bias[layer_at], my_row * out_width, out_width
        )
        mixed_out = lax.all_to_all(
            lax.all_to_all(summed, ("section", "row"), split_axis=0, concat_axis=1, tiled=True),
            "col",
            split_axis=1,
            concat_axis=0,
            tiled=True,
        )
        kept_inputs.append(gathered)
        kept_mixed.append(mixed_out)
        current = (pooled_wide * mixed_out + current.astype(jnp.float32)).astype(jnp.bfloat16)
    gradient = upstream.astype(jnp.float32)
    carried = jnp.zeros(gradient.shape, jnp.float32)
    weight_tiles = [None] * layers
    bias_tiles = [None] * layers
    pooled_grad = gradient
    full_grad = None
    for layer_at in reversed(range(layers)):
        delta_rows = (pooled_wide * gradient).astype(jnp.bfloat16)
        wide_delta = lax.all_gather(delta_rows, "col", axis=1, tiled=True)
        full_delta = lax.all_to_all(
            wide_delta, ("section", "row"), split_axis=1, concat_axis=0, tiled=True
        )
        weight_tiles[layer_at] = lax.dot_general(
            kept_inputs[layer_at],
            full_delta,
            (((0,), (0,)), ((), ())),
            preferred_element_type=jnp.float32,
        )
        bias_tiles[layer_at] = jnp.sum(full_delta, axis=0, dtype=jnp.float32)
        carried = carried + gradient * kept_mixed[layer_at]
        weight = cross_weight[layer_at]

        def back_rows(first_row, row_count, full_delta=full_delta, weight=weight):
            return lax.dot_general(
                full_delta, weight, (((1,), (1,)), ((), ())), preferred_element_type=jnp.float32
            )

        if layer_at > 0:
            gradient = gradient + lax.psum_scatter(
                back_rows(jnp.int32(0), lax.axis_size(("section", "row")) * block_rows),
                ("section", "row"),
                scatter_dimension=0,
                tiled=True,
            )
        else:
            gradient = gradient + lax.psum_scatter(
                back_rows(jnp.int32(0), block_rows * lax.axis_size(("section", "row"))).astype(
                    jnp.bfloat16
                ),
                ("section", "row"),
                scatter_dimension=0,
                tiled=True,
            ).astype(jnp.float32)
            pooled_grad = gradient + carried
            full_grad = lax.all_gather(
                pooled_grad.astype(jnp.bfloat16), ("section", "row"), axis=0, tiled=True
            )
    grad_rows_full = full_grad.reshape(batch_rows, feat_count, entry_width)
    table_grad = jnp.einsum(
        "fbv,bfe->fve", counts, grad_rows_full, preferred_element_type=jnp.float32
    )
    return (current, pooled_grad, table_grad, jnp.stack(weight_tiles), jnp.stack(bias_tiles))


def solution(mesh):
    return jax.shard_map(
        body,
        mesh=mesh,
        in_specs=(
            P("col", ("section", "row"), None),
            P(None, "col", None),
            P(None, "col", ("section", "row")),
            P(),
            P(("section", "row"), "col"),
        ),
        out_specs=(
            P(("section", "row"), "col"),
            P(("section", "row"), "col"),
            P("col", ("section", "row"), None),
            P(None, "col", ("section", "row")),
            P(None, ("section", "row")),
        ),
        check_vma=False,
    )
```

profile of v0, /device:TPU:1, one launch (start us, length us, event | category | flops | bytes accessed | tf_op | source)
XLA Modules:
  0.0 288.6 jit_solution(3041260940142367711)
XLA Ops:
  21.2 37.8 %reduce-scatter.6.cloned.1.call-done = f32[16,2048]{1,0:T(8,128)} async-done(((f32[128,2048]{1,0:T(8,128)}), f32[16,2048]{1,0:T(8,128)}) %reduce-scatter.6.cloned.1.call-update) | async-done | bytes 131088 | tf_op jit(solution)/shard_map/reduce_scatter | solution.py:33
  59.9 25.0 %all_gather.15 = bf16[128,2048]{1,0:T(8,128)(2,1)S(1)} all-gather(bf16[16,2048]{1,0:T(8,128)(2,1)S(1)} %get-tuple-element.8), channel_id=1, replica_groups=mesh['section'=2,'row'=4,'col'=4] {'section','row'}, dimensions={0}, use_global_device_ids=true | all-gather | bytes 589824 | tf_op jit(solution)/shard_map/all_gather | solution.py:46
  85.1 3.9 %fusion.2 = f32[8,4,4,1024]{3,0,2,1:T(8,128)} fusion(bf16[2,2048,1024]{2,1,0:T(8,128)(2,1)} %param.7, bf16[8,4,4,2048]{3,2,1,0:T(4,128)(2,1)S(1)} %dot_general.29), kind=kOutput, calls=%fused_computation.5 | convolution fusion | flops 536870912 | bytes 5242880 | tf_op jit(solution)/shard_map/dot_general | solution.py:47
  89.0 13.4 %all_gather.17 = bf16[16,8192]{1,0:T(8,128)(2,1)S(1)} all-gather(bf16[16,2048]{1,0:T(8,128)(2,1)S(1)} %get-tuple-element.7), channel_id=1, replica_groups=mesh['section'=2,'row'=4,'col'=4] {'col'}, dimensions={1}, use_global_device_ids=true | all-gather | bytes 327680 | tf_op jit(solution)/shard_map/all_gather | solution.py:76
  103.1 6.1 %all-to-all-start.4 = ((bf16[16,8,1024]{2,0,1:T(8,128)(2,1)}), bf16[16,8,1024]{2,0,1:T(8,128)(2,1)S(1)}, u32[]{:S(2)}, u32[]{:S(2)}) async-start(bf16[16,8,1024]{2,0,1:T(8,128)(2,1)} %bitcast.119), calls=%async_computation.7 | async-start | bytes 524288 | tf_op jit(solution)/shard_map/all_to_all | solution.py:77
  109.2 6.2 %all-to-all-done.4 = bf16[16,8,1024]{2,0,1:T(8,128)(2,1)S(1)} async-done(((bf16[16,8,1024]{2,0,1:T(8,128)(2,1)}), bf16[16,8,1024]{2,0,1:T(8,128)(2,1)S(1)}, u32[]{:S(2)}, u32[]{:S(2)}) %all-to-all-start.4) | async-done | bytes 262176 | tf_op jit(solution)/shard_map/all_to_all | solution.py:77
  115.5 4.7 %fusion.4 = f32[128,2048]{1,0:T(8,128)} fusion(bf16[128,1024]{1,0:T(8,128)(2,1)S(1)} %bitcast.121, bf16[2,2048,1024]{2,1,0:T(8,128)(2,1)} %param.7), kind=kOutput, calls=%fused_computation.7 | convolution fusion | flops 536870912 | bytes 5505024 | tf_op jit(solution)/shard_map/dot_general | solution.py:91
  121.3 7.7 %all_to_all.102 = f32[8,4,1024]{2,1,0:T(4,128)S(1)} all-to-all(f32[8,4,1024]{2,1,0:T(4,128)S(1)} %copy.165), channel_id=1, replica_groups=mesh['section'=2,'row'=4,'col'=4] {'section','row'}, dimensions={0} | all-to-all | bytes 262144 | tf_op jit(solution)/shard_map/all_to_all | solution.py:59
  129.0 9.0 %all_to_all.103 = f32[4,4,2048]{2,0,1:T(4,128)S(1)} all-to-all(f32[4,4,2048]{2,0,1:T(4,128)S(1)} %bitcast.129), channel_id=1, replica_groups=mesh['section'=2,'row'=4,'col'=4] {'col'}, dimensions={1} | all-to-all | bytes 262144 | tf_op jit(solution)/shard_map/all_to_all | solution.py:58
  138.0 17.1 %reduce-scatter.12.cloned.1.call-done = f32[16,2048]{1,0:T(8,128)} async-done(((f32[128,2048]{1,0:T(8,128)}), f32[16,2048]{1,0:T(8,128)}) %reduce-scatter.12.cloned.1.call-update) | async-done | bytes 131088 | tf_op jit(solution)/shard_map/reduce_scatter | solution.py:96
  156.1 25.2 %all_gather.16 = bf16[128,2048]{1,0:T(8,128)(2,1)S(1)} all-gather(bf16[16,2048]{1,0:T(8,128)(2,1)S(1)} %get-tuple-element.19), channel_id=1, replica_groups=mesh['section'=2,'row'=4,'col'=4] {'section','row'}, dimensions={0}, use_global_device_ids=true | all-gather | bytes 589824 | tf_op jit(solution)/shard_map/all_gather | solution.py:46
  181.5 3.9 %fusion = f32[8,4,4,1024]{3,0,2,1:T(8,128)} fusion(bf16[2,2048,1024]{2,1,0:T(8,128)(2,1)} %param.7, bf16[8,4,4,2048]{3,2,1,0:T(4,128)(2,1)S(1)} %dot_general.31), kind=kOutput, calls=%fused_computation.3 | convolution fusion | flops 536870912 | bytes 5242880 | tf_op jit(solution)/shard_map/dot_general | solution.py:47
  185.4 13.3 %all_gather.18 = bf16[16,8192]{1,0:T(8,128)(2,1)S(1)} all-gather(bf16[16,2048]{1,0:T(8,128)(2,1)S(1)} %get-tuple-element.18), channel_id=1, replica_groups=mesh['section'=2,'row'=4,'col'=4] {'col'}, dimensions={1}, use_global_device_ids=true | all-gather | bytes 327680 | tf_op jit(solution)/shard_map/all_gather | solution.py:76
  199.4 6.3 %all-to-all-start.5 = ((bf16[16,8,1024]{2,0,1:T(8,128)(2,1)}), bf16[16,8,1024]{2,0,1:T(8,128)(2,1)S(1)}, u32[]{:S(2)}, u32[]{:S(2)}) async-start(bf16[16,8,1024]{2,0,1:T(8,128)(2,1)} %bitcast.118), calls=%async_computation.9 | async-start | bytes 524288 | tf_op jit(solution)/shard_map/all_to_all | solution.py:77
  205.8 4.5 %convolution_bitcast_fusion = f32[1,2048,1024]{2,1,0:T(8,128)} fusion(bf16[128,2048]{1,0:T(8,128)(2,1)S(1)} %all_gather.16, bf16[128,1024]{1,0:T(8,128)(2,1)S(1)} %bitcast.122), kind=kOutput, calls=%fused_computation.1 | convolution fusion | flops 536870912 | bytes 9175040 | tf_op jit(solution)/shard_map/dot_general | solution.py:80
  210.3 1.7 all-to-all-done.5
  212.0 4.5 %convolution_bitcast_fusion.1 = f32[1,2048,1024]{2,1,0:T(8,128)} fusion(bf16[128,2048]{1,0:T(8,128)(2,1)S(1)} %all_gather.15, bf16[128,1024]{1,0:T(8,128)(2,1)S(1)} %bitcast.123), kind=kOutput, calls=%fused_computation.2 | convolution fusion | flops 536870912 | bytes 9175040 | tf_op jit(solution)/shard_map/dot_general | solution.py:80
  216.4 4.5 %fusion.12 = bf16[128,2048]{1,0:T(8,128)(2,1)} fusion(bf16[128,1024]{1,0:T(8,128)(2,1)S(1)} %bitcast.124, bf16[2,2048,1024]{2,1,0:T(8,128)(2,1)} %param.7), kind=kOutput, calls=%fused_computation.15 | convolution fusion | flops 537133056 | bytes 4980736 | tf_op jit(solution)/shard_map/dot_general | solution.py:91
  222.7 4.2 %all-to-all-start.2 = ((f32[8,4,1024]{2,1,0:T(4,128)}), f32[8,4,1024]{2,1,0:T(4,128)}, u32[]{:S(2)}, u32[]{:S(2)}) async-start(f32[8,4,1024]{2,1,0:T(4,128)} %copy.167), calls=%async_computation.5 | async-start | bytes 262144 | tf_op jit(solution)/shard_map/all_to_all | solution.py:59
  226.9 12.2 %pad_maximum_fusion = f32[2,2048,1024]{2,1,0:T(8,128)} fusion(f32[1,2048,1024]{2,1,0:T(8,128)} %convolution_bitcast_fusion, f32[1,2048,1024]{2,1,0:T(8,128)} %convolution_bitcast_fusion.1), kind=kLoop, calls=%fused_computation | loop fusion | flops 4194304 | bytes 33554432 | tf_op jit(solution)/shard_map/stack | solution.py:119
  239.1 4.6 %all-to-all-start.3 = ((f32[4,4,2048]{2,0,1:T(4,128)}), f32[4,4,2048]{2,0,1:T(4,128)S(1)}, u32[]{:S(2)}, u32[]{:S(2)}) async-start(f32[4,4,2048]{2,0,1:T(4,128)} %bitcast.32), calls=%async_computation.6 | async-start | bytes 262144 | tf_op jit(solution)/shard_map/all_to_all | solution.py:58
  244.3 4.2 %all-to-all-done.3 = f32[4,4,2048]{2,0,1:T(4,128)S(1)} async-done(((f32[4,4,2048]{2,0,1:T(4,128)}), f32[4,4,2048]{2,0,1:T(4,128)S(1)}, u32[]{:S(2)}, u32[]{:S(2)}) %all-to-all-start.3) | async-done | bytes 131104 | tf_op jit(solution)/shard_map/all_to_all | solution.py:58
  248.6 5.5 %reduce-scatter.14.cloned.1.call-done = bf16[16,2048]{1,0:T(8,128)(2,1)} async-done(((bf16[128,2048]{1,0:T(8,128)(2,1)}), bf16[16,2048]{1,0:T(8,128)(2,1)}) %reduce-scatter.14.cloned.1.call-update) | async-done | bytes 65552 | tf_op jit(solution)/shard_map/reduce_scatter | solution.py:103
  255.7 25.1 %all_gather.19 = bf16[128,2048]{1,0:T(8,128)(2,1)S(1)} all-gather(bf16[16,2048]{1,0:T(8,128)(2,1)S(1)} %get-tuple-element.5), channel_id=1, replica_groups=mesh['section'=2,'row'=4,'col'=4] {'section','row'}, dimensions={0}, use_global_device_ids=true | all-gather | bytes 589824 | tf_op jit(solution)/shard_map/all_gather | solution.py:112
  (122 shorter events, 24.0 us)
Async XLA Ops:
  7.2 12.0 %copy-start = (bf16[8,128,256]{2,1,0:T(8,128)(2,1)S(1)}, bf16[8,128,256]{2,1,0:T(8,128)(2,1)}, u32[]{:S(2)}) copy-start(bf16[8,128,256]{2,1,0:T(8,128)(2,1)} %param.5) | copy-start | bytes 1572868
  7.2 51.8 %copy-start.1 = (bf16[16,2048]{1,0:T(8,128)(2,1)S(1)}, bf16[16,2048]{1,0:T(8,128)(2,1)}, u32[]{:S(2)}) copy-start(bf16[16,2048]{1,0:T(8,128)(2,1)} %param.9) | copy-start | bytes 196612
  7.2 51.8 %reduce-scatter.6.cloned.1.call-start = ((), (), s32[]{:S(2)}) async-start(), calls=%async_computation.11 | async-start | bytes 1179648 | tf_op jit(solution)/shard_map/reduce_scatter | solution.py:33
  21.1 99.2 %reduce-scatter.8.cloned.1.call-start = ((), (), s32[]{:S(2)}) async-start(), calls=%async_computation.12 | async-start | bytes 655360 | tf_op jit(solution)/shard_map/reduce_scatter | solution.py:52
  85.1 35.2 %copy-start.3 = (f32[2,8192]{1,0:T(2,128)S(1)}, f32[2,8192]{1,0:T(2,128)}, u32[]{:S(2)}) copy-start(f32[2,8192]{1,0:T(2,128)} %param.8) | copy-start | bytes 196612
  103.1 12.3 %all-to-all-start.4 = ((bf16[16,8,1024]{2,0,1:T(8,128)(2,1)}), bf16[16,8,1024]{2,0,1:T(8,128)(2,1)S(1)}, u32[]{:S(2)}, u32[]{:S(2)}) async-start(bf16[16,8,1024]{2,0,1:T(8,128)(2,1)} %bitcast.119), calls=%async_computation.7 | async-start | bytes 524288 | tf_op jit(solution)/shard_map/all_to_all | solution.py:77
  109.2 45.9 %reduce-scatter.12.cloned.1.call-start = ((), (), s32[]{:S(2)}) async-start(), calls=%async_computation.14 | async-start | bytes 1179648 | tf_op jit(solution)/shard_map/reduce_scatter | solution.py:96
  120.2 100.8 %reduce-scatter.10.cloned.1.call-start = ((), (), s32[]{:S(2)}) async-start(), calls=%async_computation.13 | async-start | bytes 655360 | tf_op jit(solution)/shard_map/reduce_scatter | solution.py:52
  199.4 12.5 %all-to-all-start.5 = ((bf16[16,8,1024]{2,0,1:T(8,128)(2,1)}), bf16[16,8,1024]{2,0,1:T(8,128)(2,1)S(1)}, u32[]{:S(2)}, u32[]{:S(2)}) async-start(bf16[16,8,1024]{2,0,1:T(8,128)(2,1)} %bitcast.118), calls=%async_computation.9 | async-start | bytes 524288 | tf_op jit(solution)/shard_map/all_to_all | solution.py:77
  205.7 48.4 %reduce-scatter.14.cloned.1.call-start = ((), (), s32[]{:S(2)}) async-start(), calls=%async_computation.15 | async-start | bytes 589824 | tf_op jit(solution)/shard_map/reduce_scatter | solution.py:103
  222.7 16.4 %all-to-all-start.2 = ((f32[8,4,1024]{2,1,0:T(4,128)}), f32[8,4,1024]{2,1,0:T(4,128)}, u32[]{:S(2)}, u32[]{:S(2)}) async-start(f32[8,4,1024]{2,1,0:T(4,128)} %copy.167), calls=%async_computation.5 | async-start | bytes 262144 | tf_op jit(solution)/shard_map/all_to_all | solution.py:59
  226.9 27.2 %copy-start.2 = (f32[16,2048]{1,0:T(8,128)S(1)}, f32[16,2048]{1,0:T(8,128)}, u32[]{:S(2)}) copy-start(f32[16,2048]{1,0:T(8,128)} %reduce-scatter.12.cloned.1.call-done) | copy-start | bytes 393220
  239.1 9.5 %all-to-all-start.3 = ((f32[4,4,2048]{2,0,1:T(4,128)}), f32[4,4,2048]{2,0,1:T(4,128)S(1)}, u32[]{:S(2)}, u32[]{:S(2)}) async-start(f32[4,4,2048]{2,0,1:T(4,128)} %bitcast.32), calls=%async_computation.6 | async-start | bytes 262144 | tf_op jit(solution)/shard_map/all_to_all | solution.py:58
Sparse Core Ops, SparseCore 0:
  21.2 37.6 reduce-scatter.5
  89.2 20.9 reduce-scatter.7
  120.3 34.8 reduce-scatter.11
  185.5 20.9 reduce-scatter.9
  221.1 32.9 reduce-scatter.13
where the time goes:
time: 290 us; the launch traced here: 289 us
  blocking collectives  119 us (41%)
  waiting for transfers between devices  72.6 us (25%)
  matrix products  27.6 us (10%)
  other arithmetic  26.5 us (9%)
  starting transfers between devices  21.3 us (7%)
  between operations  14.2 us (5%)
  local copies, waits for them, and re-layouts  7.78 us (3%)
    all_gather x2, blocking collectives, body(): gathered = lax.all_gather(current, ('section', 'row'), axis=0, tiled=True)  50.2 us
    reduce_scatter x1, waiting for transfers between devices, body(): lax.psum_scatter(pooled_part.reshape(lax.axis_size(('section', 'row')) *...  37.8 us
    all_gather x2, blocking collectives, body(): wide_delta = lax.all_gather(delta_rows, 'col', axis=1, tiled=True)  26.7 us
    all_gather x1, blocking collectives, body(): lax.all_gather(pooled_grad.astype(jnp.bfloat16), ('section', 'row'), axis...  25.1 us
    reduce_scatter x1, waiting for transfers between devices, body(): lax.psum_scatter(back_rows(jnp.int32(0), lax.axis_size(('section', 'row')...  17.1 us
    all_to_all x2, starting transfers between devices, body(): lax.all_to_all(wide_delta, ('section', 'row'), split_axis=1, concat_axis=...  12.4 us
    another operation x1, other arithmetic, body(): jnp.stack(weight_tiles)  12.2 us
    dot_general x2, matrix products, back_rows(): lax.dot_general(full_delta, weight, (((1,), (1,)), ((), ())), preferred_e...  9.16 us
  transfers between devices with their start and end apart: 9, of which 6 were waited for; matrix products, arithmetic and copies ran while one was open for 12% of the time, Pallas kernels for 0%

commit v1 on v0

v1 whole, which is shorter than its diff:
```python
import functools
import math

import jax
import jax.numpy as jnp
from jax import lax
from jax.experimental import pallas as pl
from jax.experimental.pallas import tpu as pltpu
from jax.sharding import PartitionSpec as P

MESH = pl.DeviceIdType.MESH


def bag_counts(local_ids, shard_rows):
    slot_ids = lax.broadcasted_iota(jnp.int32, (1, 1, shard_rows), 2)
    bag_len = local_ids.shape[1]
    group_size = math.gcd(bag_len, 8)
    summed = jnp.zeros((local_ids.shape[0], shard_rows), jnp.float32)
    for offset in range(0, bag_len, group_size):
        matches = local_ids[:, offset : offset + group_size, None] == slot_ids
        summed = summed + jnp.sum(matches, axis=1, dtype=jnp.float32)
    return summed.astype(jnp.bfloat16)


def tile_of(width):
    return math.gcd(width, 256)


def kernel(
    sizes,
    counts,
    tables,
    up,
    bias,
    w_hbm,
    xa_out,
    db_out,
    crossed_out,
    pgrad_out,
    ga_out,
    w,
    part,
    pr,
    xa,
    db,
    ga,
    drow,
    mpart,
    mr,
    gpart,
    gr,
    mixed,
    w_sem,
    rs_send,
    rs_recv,
    ag_send,
    ag_recv,
    b_send,
    b_recv,
    m_send,
    m_recv,
    g_send,
    g_recv,
):
    section_count, row_count, C = sizes
    N = section_count * row_count
    L, IW, OW = w.shape
    B = xa.shape[1]
    R = B // N
    r = IW // OW
    feats, _, entry = tables.shape
    n = lax.axis_index("section") * row_count + lax.axis_index("row")
    c = lax.axis_index("col")
    home = n // r
    half = n % r

    def device(np_at, col_at):
        return (np_at // row_count, np_at % row_count, col_at)

    def rows_of(np_at):
        return pl.ds(pl.multiple_of(np_at * R, R), R)

    my_rows = rows_of(n)

    barrier = pltpu.get_barrier_semaphore()
    total = N * C
    me = n * C + c

    @pl.loop(1, total)
    def _(d):
        other = lax.rem(me + d, total)
        pl.semaphore_signal(
            barrier, inc=1, device_id=device(other // C, other % C), device_id_type=MESH
        )

    loads = []
    for layer in range(L):
        load = pltpu.make_async_copy(w_hbm.at[layer], w.at[layer], w_sem.at[layer])
        load.start()
        loads.append(load)

    for f in range(feats):
        part[:, f * entry : (f + 1) * entry] = jnp.dot(
            counts[f], tables[f], preferred_element_type=jnp.float32
        ).astype(jnp.bfloat16)

    pl.semaphore_wait(barrier, total - 1)

    sent = []

    def scatter_plane(src, dst, send_sem, recv_sem):
        copies = []
        for d in range(1, N):
            to = lax.rem(n + d, N)
            copy = pltpu.make_async_remote_copy(
                src_ref=src.at[rows_of(to)],
                dst_ref=dst.at[d],
                send_sem=send_sem.at[d],
                recv_sem=recv_sem.at[d],
                device_id=device(to, c),
                device_id_type=MESH,
            )
            copy.start()
            copies.append(copy)
        sent.extend(copies)
        return copies

    def sum_plane(copies, src, dst):
        value = src[my_rows, :].astype(jnp.float32)
        for d in range(1, N):
            copies[d - 1].wait_recv()
            value = value + dst[d].astype(jnp.float32)
        return value

    def gather_plane(buf, send_sem, recv_sem):
        copies = []
        for d in range(1, N):
            to = lax.rem(n + d, N)
            copy = pltpu.make_async_remote_copy(
                src_ref=buf.at[my_rows],
                dst_ref=buf.at[my_rows],
                send_sem=send_sem.at[d],
                recv_sem=recv_sem.at[d],
                device_id=device(to, c),
                device_id_type=MESH,
            )
            copy.start()
            copies.append(copy)
        sent.extend(copies)
        return copies

    def wait_plane(copies):
        for copy in copies:
            copy.wait_recv()

    finals = []

    def send_to_features(rows, buf, send_sem, recv_sem):
        for h in range(r):
            for dc in range(C):
                src = rows.at[:, h * OW : (h + 1) * OW]
                to_np = c * r + h
                to_c = lax.rem(c + dc, C)
                copy = pltpu.make_async_remote_copy(
                    src_ref=src,
                    dst_ref=buf.at[my_rows],
                    send_sem=send_sem.at[h * C + dc],
                    recv_sem=recv_sem.at[n],
                    device_id=device(to_np, to_c),
                    device_id_type=MESH,
                )
                if dc == 0:
                    mine = to_np == n

                    @pl.when(mine)
                    def _():
                        pltpu.make_async_copy(src, buf.at[my_rows], recv_sem.at[n]).start()

                    @pl.when(jnp.logical_not(mine))
                    def _():
                        copy.start()

                    finals.append((jnp.logical_not(mine), copy))
                else:
                    copy.start()
                    sent.append(copy)

    def wait_features(buf, recv_sem):
        for s in range(N):
            piece = buf.at[s * R : (s + 1) * R]
            pltpu.make_async_copy(piece, piece, recv_sem.at[s]).wait()

    def send_to_rows(src, dst, send_sem, recv_sem):
        slot = half * C + c
        for dn in range(N):
            to = lax.rem(n + dn, N)
            copy = pltpu.make_async_remote_copy(
                src_ref=src.at[rows_of(to)],
                dst_ref=dst.at[slot],
                send_sem=send_sem.at[dn],
                recv_sem=recv_sem.at[slot],
                device_id=device(to, home),
                device_id_type=MESH,
            )
            if dn == 0:
                mine = c == home

                @pl.when(mine)
                def _():
                    pltpu.make_async_copy(
                        src.at[my_rows], dst.at[slot], recv_sem.at[slot]
                    ).start()

                @pl.when(jnp.logical_not(mine))
                def _():
                    copy.start()

                finals.append((jnp.logical_not(mine), copy))
            else:
                copy.start()
                sent.append(copy)

    def wait_rows(dst, recv_sem):
        for slot in range(r * C):
            piece = dst.at[slot]
            pltpu.make_async_copy(piece, piece, recv_sem.at[slot]).wait()

    first = scatter_plane(part, pr, rs_send, rs_recv)
    pooled = sum_plane(first, part, pr).astype(jnp.bfloat16)
    xa[0, my_rows, :] = pooled
    gathers = gather_plane(xa.at[0], ag_send.at[0], ag_recv.at[0])
    pooled_wide = pooled.astype(jnp.float32)
    gradient = up[...].astype(jnp.float32)
    drow[L - 1] = (pooled_wide * gradient).astype(jnp.bfloat16)
    send_to_features(drow.at[L - 1], db.at[L - 1], b_send.at[L - 1], b_recv.at[L - 1])
    current = pooled
    carried = jnp.zeros(gradient.shape, jnp.float32)
    for load in loads:
        load.wait()
    kept = [None] * (L + 1)
    kept[L] = gradient
    for step in range(L):
        back = L - 1 - step
        wait_plane(gathers)
        tile = tile_of(OW)

        @pl.loop(0, OW // tile)
        def _(at):
            cols = pl.ds(pl.multiple_of(at * tile, tile), tile)
            mpart[step, :, cols] = jnp.dot(
                xa[step], w[step, :, cols], preferred_element_type=jnp.float32
            ).astype(jnp.bfloat16)

        send_to_rows(mpart.at[step], mr.at[step], m_send.at[step], m_recv.at[step])
        wait_features(db.at[back], b_recv.at[back])
        wide = tile_of(IW)

        @pl.loop(0, IW // wide)
        def _(at):
            cols = pl.ds(pl.multiple_of(at * wide, wide), wide)
            gpart[back, :, cols] = lax.dot_general(
                db[back],
                w[back, cols, :],
                (((1,), (1,)), ((), ())),
                preferred_element_type=jnp.float32,
            ).astype(jnp.bfloat16)

        sums = scatter_plane(gpart.at[back], gr.at[back], g_send.at[back], g_recv.at[back])
        xa_out[step] = xa[step]
        db_out[back] = db[back]
        wait_rows(mr.at[step], m_recv.at[step])
        for h in range(r):
            value = mr[step, h * C].astype(jnp.float32)
            for col_at in range(1, C):
                value = value + mr[step, h * C + col_at].astype(jnp.float32)
            mixed[step, :, h * OW : (h + 1) * OW] = value
        mixed[step] = mixed[step] + bias[step : step + 1, :]
        current = (pooled_wide * mixed[step] + current.astype(jnp.float32)).astype(jnp.bfloat16)
        if step + 1 < L:
            xa[step + 1, my_rows, :] = current
            gathers = gather_plane(xa.at[step + 1], ag_send.at[step + 1], ag_recv.at[step + 1])
        else:
            crossed_out[...] = current
        kept[back] = kept[back + 1] + sum_plane(sums, gpart.at[back], gr.at[back])
        if back > 0:
            drow[back - 1] = (pooled_wide * kept[back]).astype(jnp.bfloat16)
            send_to_features(
                drow.at[back - 1], db.at[back - 1], b_send.at[back - 1], b_recv.at[back - 1]
            )
    pooled_grad = kept[0]
    for layer in range(L):
        carried = carried + kept[layer + 1] * mixed[layer]
    pooled_grad = kept[0] + carried
    pgrad_out[...] = pooled_grad
    ga[my_rows, :] = pooled_grad.astype(jnp.bfloat16)
    gathers = gather_plane(ga, ag_send.at[L], ag_recv.at[L])
    for copy in sent[: -(N - 1)]:
        copy.wait_send()
    for remote, copy in finals:

        @pl.when(remote)
        def _(copy=copy):
            copy.wait_send()

    wait_plane(gathers)
    ga_out[...] = ga[...]
    for copy in sent[-(N - 1) :]:
        copy.wait_send()


def body(tables, bag_index, cross_weight, cross_bias, upstream):
    feat_count, shard_rows, entry_width = tables.shape
    batch_rows = bag_index.shape[0]
    layers, in_width, out_width = cross_weight.shape
    block_rows = upstream.shape[0]
    sizes = tuple(lax.axis_size(axis) for axis in ("section", "row", "col"))
    np_count = sizes[0] * sizes[1]
    col_count = sizes[2]
    ratio = in_width // out_width
    my_row = lax.axis_index(("section", "row"))
    local_ids = bag_index - my_row * shard_rows
    counts = jnp.stack(
        [bag_counts(local_ids[:, feature_at, :], shard_rows) for feature_at in range(feat_count)]
    )
    bias = lax.dynamic_slice_in_dim(cross_bias, lax.axis_index("col") * in_width, in_width, axis=1)
    bf16, f32 = jnp.bfloat16, jnp.float32
    vmem = pl.BlockSpec(memory_space=pltpu.VMEM)
    dma = pltpu.SemaphoreType.DMA
    xa, db, crossed, pooled_grad, full_grad = pl.pallas_call(
        functools.partial(kernel, sizes),
        out_shape=(
            jax.ShapeDtypeStruct((layers, batch_rows, in_width), bf16),
            jax.ShapeDtypeStruct((layers, batch_rows, out_width), bf16),
            jax.ShapeDtypeStruct((block_rows, in_width), bf16),
            jax.ShapeDtypeStruct((block_rows, in_width), f32),
            jax.ShapeDtypeStruct((batch_rows, in_width), bf16),
        ),
        in_specs=[vmem, vmem, vmem, vmem, pl.BlockSpec(memory_space=pl.ANY)],
        out_specs=(vmem,) * 5,
        scratch_shapes=[
            pltpu.VMEM((layers, in_width, out_width), bf16),
            pltpu.VMEM((batch_rows, in_width), bf16),
            pltpu.VMEM((np_count, block_rows, in_width), bf16),
            pltpu.VMEM((layers, batch_rows, in_width), bf16),
            pltpu.VMEM((layers, batch_rows, out_width), bf16),
            pltpu.VMEM((batch_rows, in_width), bf16),
            pltpu.VMEM((layers, block_rows, in_width), bf16),
            pltpu.VMEM((layers, batch_rows, out_width), bf16),
            pltpu.VMEM((layers, ratio * col_count, block_rows, out_width), bf16),
            pltpu.VMEM((layers, batch_rows, in_width), bf16),
            pltpu.VMEM((layers, np_count, block_rows, in_width), bf16),
            pltpu.VMEM((layers, block_rows, in_width), f32),
            dma((layers,)),
            dma((np_count,)),
            dma((np_count,)),
            dma((layers + 1, np_count)),
            dma((layers + 1, np_count)),
            dma((layers, ratio * col_count)),
            dma((layers, np_count)),
            dma((layers, np_count)),
            dma((layers, ratio * col_count)),
            dma((layers, np_count)),
            dma((layers, np_count)),
        ],
        compiler_params=pltpu.CompilerParams(
            collective_id=0, has_side_effects=True, vmem_limit_bytes=56 * 1024 * 1024
        ),
    )(counts, tables, upstream, bias, cross_weight)
    weight_grad = jnp.einsum("lbi,lbo->lio", xa, db, preferred_element_type=f32)
    bias_grad = jnp.sum(db, axis=1, dtype=f32)
    grad_rows_full = full_grad.reshape(batch_rows, feat_count, entry_width)
    table_grad = jnp.einsum("fbv,bfe->fve", counts, grad_rows_full, preferred_element_type=f32)
    return crossed, pooled_grad, table_grad, weight_grad, bias_grad


def solution(mesh):
    return jax.shard_map(
        body,
        mesh=mesh,
        in_specs=(
            P("col", ("section", "row"), None),
            P(None, "col", None),
            P(None, "col", ("section", "row")),
            P(),
            P(("section", "row"), "col"),
        ),
        out_specs=(
            P(("section", "row"), "col"),
            P(("section", "row"), "col"),
            P("col", ("section", "row"), None),
            P(None, "col", ("section", "row")),
            P(None, ("section", "row")),
        ),
        check_vma=False,
    )
```

time: 290 us -> 102 us (0.35)
  blocking collectives: 119 us -> 0 us
  Pallas kernels: 0 us -> 74.8 us
  waiting for transfers between devices: 72.6 us -> 0 us
  starting transfers between devices: 21.3 us -> 0 us
  other arithmetic: 26.5 us -> 9.04 us
  matrix products: 27.6 us -> 11.3 us
  between operations: 14.2 us -> 0.99 us
    all_gather x5 -> x0, blocking collectives: 102 us -> none  [the longest x2 50.2 us: body(): gathered = lax.all_gather(current, ('section', 'row'), axis=0, tiled=True)]
    pallas_call x0 -> x1, Pallas kernels: none -> 74.8 us  [body(): pl.pallas_call(functools.partial(kernel, sizes), out_shape=(jax.ShapeDtyp...]
    reduce_scatter x5 -> x0, waiting for transfers between devices: 60.4 us -> none  [the longest x1 37.8 us: body(): lax.psum_scatter(pooled_part.reshape(lax.axis_size(('section', 'row')) *...]
    all_to_all x4 -> x0, starting transfers between devices: 21.2 us -> none  [the longest x2 12.4 us: body(): lax.all_to_all(wide_delta, ('section', 'row'), split_axis=1, concat_axis=...]
    all_to_all x2 -> x0, blocking collectives: 16.7 us -> none  [the longest x1 9 us: body(): lax.all_to_all(lax.all_to_all(summed, ('section', 'row'), split_axis=0, c...]
    dot_general x7 -> x1, matrix products: 26.3 us -> 10 us  [body(): weight_grad = jnp.einsum('lbi,lbo->lio', xa, db, preferred_element_type=f32)]
    another operation x2 -> x0, other arithmetic: 12.8 us -> none  [the longest x1 12.2 us: body(): jnp.stack(weight_tiles)]
    all_to_all x4 -> x0, waiting for transfers between devices: 12.1 us -> none  [the longest x2 7.91 us: body(): lax.all_to_all(wide_delta, ('section', 'row'), split_axis=1, concat_axis=...]
  transfers between devices with their start and end apart: 9 -> 0, of which waited for: 6 -> 0; matrix products, arithmetic and copies ran while one was open for 12% -> 0% of each run, Pallas kernels for 0% -> 0%
where the time goes in v1:
time: 102 us; the launch traced here: 101 us
  Pallas kernels  74.8 us (73%)
  matrix products  11.3 us (11%)
  other arithmetic  9.04 us (9%)
  local copies, waits for them, and re-layouts  5.29 us (5%)
    pallas_call x1, Pallas kernels, body(): pl.pallas_call(functools.partial(kernel, sizes), out_shape=(jax.ShapeDtyp...  74.8 us
    dot_general x1, matrix products, body(): weight_grad = jnp.einsum('lbi,lbo->lio', xa, db, preferred_element_type=f32)  10 us
    reduce_sum x32, other arithmetic, bag_counts(): summed = summed + jnp.sum(matches, axis=1, dtype=jnp.float32)  7.18 us
    slice x36, local copies, waits for them, and re-layouts, bag_counts(): matches = local_ids[:, offset:offset + group_size, None] == slot_ids  3.28 us

profile of v1, /device:TPU:1, one launch (start us, length us, event | category | flops | bytes accessed | tf_op | source)
XLA Modules:
  0.0 101.4 jit_solution(927644623605823805)
XLA Ops:
  0.7 0.9 broadcast_subtract_fusion
  2.1 0.2 convert_reduce_fusion.30
  2.4 0.2 convert_reduce_fusion.31
  2.7 0.2 convert_reduce_fusion.32
  3.1 0.2 convert_reduce_fusion.25
  4.1 0.2 convert_reduce_fusion.28
  4.5 0.2 convert_reduce_fusion.21
  5.1 0.2 convert_reduce_fusion.23
  5.5 0.2 convert_reduce_fusion.24
  6.2 0.2 convert_reduce_fusion.18
  6.5 0.2 convert_reduce_fusion.19
  6.8 0.2 convert_reduce_fusion.20
  7.2 0.2 convert_reduce_fusion.13
  8.2 0.2 convert_reduce_fusion.16
  9.6 0.2 convert_reduce_fusion.9
  10.9 0.2 convert_reduce_fusion.8
  12.3 0.2 convert_reduce_fusion.4
  12.6 0.7 constant_dynamic-slice_fusion.bias
  13.3 74.8 %shard_map.92 = (bf16[2,128,2048]{2,1,0:T(8,128)(2,1)}, bf16[2,128,1024]{2,1,0:T(8,128)(2,1)}, bf16[16,2048]{1,0:T(8,128)(2,1)}, f32[16,2048]{1,0:T(8,128)}, bf16[128,2048]{1,0:T(8,128)(2,1)}) custom-call(bf16[8,128,128]{2,1,0:T(8,128)(2,1)} %copy-done.2, bf16[8,128,256]{2,1,0:T(8,128)(2,1)} %tables.1, bf16[16,2048]{1,0:T(8,128)(2,1)} %up.1, ...), custom_call_target="tpu_custom_call" | custom-call | tf_op jit(solution)/shard_map/pallas_call | solution.py:329
  88.1 10.0 %fusion.27 = f32[2,2048,1024]{2,1,0:T(8,128)} fusion(bf16[2,128,2048]{2,1,0:T(8,128)(2,1)} %get-tuple-element.13, bf16[2,128,1024]{2,1,0:T(8,128)(2,1)} %get-tuple-element.14), kind=kOutput, calls=%fused_computation.110 | convolution fusion | flops 1073741824 | bytes 18350080 | tf_op jit(solution)/shard_map/lbi,lbo->lio/dot_general | solution.py:369
  98.1 1.3 %fusion = f32[8,128,256]{2,1,0:T(8,128)} fusion(bf16[8,128,128]{2,1,0:T(8,128)(2,1)S(1)} %copy-done.3, bf16[16,8,8,256]{3,2,1,0:T(8,128)(2,1)S(1)} %bitcast.55), kind=kOutput, calls=%fused_computation.1 | convolution fusion | flops 67108864 | bytes 1835008 | tf_op jit(solution)/shard_map/fbv,bfe->fve/dot_general | solution.py:372
  99.4 0.7 convert_reduce_fusion
  100.1 0.6 copy.96
  100.8 0.7 copy.97
  (75 shorter events, 7.1 us)
Async XLA Ops:
  0.6 11.9 %copy-start = (f32[2,8192]{1,0:T(2,128)S(1)}, f32[2,8192]{1,0:T(2,128)}, u32[]{:S(2)}) copy-start(f32[2,8192]{1,0:T(2,128)} %param.8) | copy-start | bytes 196612
  12.6 0.7 copy-start.2
  88.0 10.1 %copy-start.3 = (bf16[8,128,128]{2,1,0:T(8,128)(2,1)S(1)}, bf16[8,128,128]{2,1,0:T(8,128)(2,1)}, u32[]{:S(2)}) copy-start(bf16[8,128,128]{2,1,0:T(8,128)(2,1)} %copy-done.2) | copy-start | bytes 786436
  88.1 10.0 %copy-start.4 = (bf16[128,2048]{1,0:T(8,128)(2,1)S(1)}, bf16[128,2048]{1,0:T(8,128)(2,1)}, u32[]{:S(2)}) copy-start(bf16[128,2048]{1,0:T(8,128)(2,1)} %get-tuple-element.12) | copy-start | bytes 1572868
  88.1 11.4 %copy-start.1 = (bf16[2,128,1024]{2,1,0:T(8,128)(2,1)S(1)}, bf16[2,128,1024]{2,1,0:T(8,128)(2,1)}, u32[]{:S(2)}) copy-start(bf16[2,128,1024]{2,1,0:T(8,128)(2,1)} %get-tuple-element.14) | copy-start | bytes 1572868
  88.1 12.0 %copy-start.6 = (bf16[16,2048]{1,0:T(8,128)(2,1)S(1)}, bf16[16,2048]{1,0:T(8,128)(2,1)}, u32[]{:S(2)}) copy-start(bf16[16,2048]{1,0:T(8,128)(2,1)} %get-tuple-element.76) | copy-start | bytes 196612
  88.1 12.7 %copy-start.5 = (f32[16,2048]{1,0:T(8,128)S(1)}, f32[16,2048]{1,0:T(8,128)}, u32[]{:S(2)}) copy-start(f32[16,2048]{1,0:T(8,128)} %get-tuple-element.77) | copy-start | bytes 393220

commit v2 on v1

--- a/solution.py
+++ b/solution.py
@@ -11,28 +11,18 @@
 MESH = pl.DeviceIdType.MESH
 
 
-def bag_counts(local_ids, shard_rows):
-    slot_ids = lax.broadcasted_iota(jnp.int32, (1, 1, shard_rows), 2)
-    bag_len = local_ids.shape[1]
-    group_size = math.gcd(bag_len, 8)
-    summed = jnp.zeros((local_ids.shape[0], shard_rows), jnp.float32)
-    for offset in range(0, bag_len, group_size):
-        matches = local_ids[:, offset : offset + group_size, None] == slot_ids
-        summed = summed + jnp.sum(matches, axis=1, dtype=jnp.float32)
-    return summed.astype(jnp.bfloat16)
-
-
 def tile_of(width):
     return math.gcd(width, 256)
 
 
 def kernel(
     sizes,
-    counts,
+    ids,
     tables,
     up,
     bias,
     w_hbm,
+    counts_out,
     xa_out,
     db_out,
     crossed_out,
@@ -41,6 +31,7 @@
     w,
     part,
     pr,
+    pair,
     xa,
     db,
     ga,
@@ -68,7 +59,10 @@
     B = xa.shape[1]
     R = B // N
     r = IW // OW
-    feats, _, entry = tables.shape
+    feats, shard_rows, entry = tables.shape
+    bag_len = ids.shape[1]
+    my_section = lax.axis_index("section")
+    my_row = lax.axis_index("row")
     n = lax.axis_index("section") * row_count + lax.axis_index("row")
     c = lax.axis_index("col")
     home = n // r
@@ -99,58 +93,115 @@
         load.start()
         loads.append(load)
 
-    for f in range(feats):
-        part[:, f * entry : (f + 1) * entry] = jnp.dot(
-            counts[f], tables[f], preferred_element_type=jnp.float32
+    slots = lax.broadcasted_iota(jnp.int32, (shard_rows, B), 0) + n * shard_rows
+
+    @pl.loop(0, feats)
+    def _(f):
+        hits = jnp.zeros((shard_rows, B), jnp.int32)
+        for j in range(bag_len):
+            hits = hits + jnp.where(ids[f, j : j + 1, :] == slots, 1, 0)
+        counts = hits.astype(jnp.float32).astype(jnp.bfloat16)
+        counts_out[f] = counts
+        cols = pl.ds(pl.multiple_of(f * entry, entry), entry)
+        part[:, cols] = lax.dot_general(
+            counts, tables[f], (((0,), (0,)), ((), ())), preferred_element_type=jnp.float32
         ).astype(jnp.bfloat16)
 
     pl.semaphore_wait(barrier, total - 1)
 
     sent = []
 
-    def scatter_plane(src, dst, send_sem, recv_sem):
-        copies = []
-        for d in range(1, N):
-            to = lax.rem(n + d, N)
-            copy = pltpu.make_async_remote_copy(
-                src_ref=src.at[rows_of(to)],
-                dst_ref=dst.at[d],
-                send_sem=send_sem.at[d],
-                recv_sem=recv_sem.at[d],
-                device_id=device(to, c),
-                device_id_type=MESH,
+    def remote(src, dst, send_sem, recv_sem, section, row):
+        copy = pltpu.make_async_remote_copy(
+            src_ref=src,
+            dst_ref=dst,
+            send_sem=send_sem,
+            recv_sem=recv_sem,
+            device_id=(section, row, c),
+            device_id_type=MESH,
+        )
+        copy.start()
+        sent.append(copy)
+        return copy
+
+    row_order = list(range(1, row_count)) + [0]
+
+    def scatter_plane(src, dst, pairs, send_sem, recv_sem):
+        twins = {}
+        for dr in row_order:
+            row = lax.rem(my_row + dr, row_count)
+            for ds in range(1, section_count):
+                at = ds * row_count + dr
+                section = lax.rem(my_section + ds, section_count)
+                twins[at] = remote(
+                    src.at[rows_of(section * row_count + row)],
+                    dst.at[at],
+                    send_sem.at[at],
+                    recv_sem.at[at],
+                    section,
+                    my_row,
+                )
+        return src, dst, pairs, send_sem, recv_sem, twins
+
+    def with_twins(scatter, dr):
+        src, dst, _, _, _, twins = scatter
+        row = lax.rem(my_row + dr, row_count)
+        value = src[rows_of(my_section * row_count + row), :].astype(jnp.float32)
+        for ds in range(1, section_count):
+            at = ds * row_count + dr
+            twins[at].wait_recv()
+            value = value + dst[at].astype(jnp.float32)
+        return value
+
+    def relay_plane(scatter):
+        _, dst, pairs, send_sem, recv_sem, _ = scatter
+        across = []
+        for dr in range(1, row_count):
+            pairs[dr] = with_twins(scatter, dr).astype(jnp.bfloat16)
+            row = lax.rem(my_row + dr, row_count)
+            across.append(
+                remote(
+                    pairs.at[dr], dst.at[dr], send_sem.at[dr], recv_sem.at[dr], my_section, row
+                )
             )
-            copy.start()
-            copies.append(copy)
-        sent.extend(copies)
-        return copies
-
-    def sum_plane(copies, src, dst):
-        value = src[my_rows, :].astype(jnp.float32)
-        for d in range(1, N):
-            copies[d - 1].wait_recv()
-            value = value + dst[d].astype(jnp.float32)
+        return scatter, across
+
+    def sum_plane(relayed):
+        scatter, across = relayed
+        value = with_twins(scatter, 0)
+        for dr in range(1, row_count):
+            across[dr - 1].wait_recv()
+            value = value + scatter[1][dr].astype(jnp.float32)
         return value
 
     def gather_plane(buf, send_sem, recv_sem):
-        copies = []
-        for d in range(1, N):
-            to = lax.rem(n + d, N)
-            copy = pltpu.make_async_remote_copy(
-                src_ref=buf.at[my_rows],
-                dst_ref=buf.at[my_rows],
-                send_sem=send_sem.at[d],
-                recv_sem=recv_sem.at[d],
-                device_id=device(to, c),
-                device_id_type=MESH,
+        across = []
+        mine = buf.at[my_rows]
+        for dr in range(1, row_count):
+            row = lax.rem(my_row + dr, row_count)
+            across.append(
+                remote(mine, mine, send_sem.at[dr], recv_sem.at[dr], my_section, row)
             )
-            copy.start()
-            copies.append(copy)
-        sent.extend(copies)
-        return copies
-
-    def wait_plane(copies):
-        for copy in copies:
+        waits = []
+        for ds in range(1, section_count):
+            at = ds * row_count
+            section = lax.rem(my_section + ds, section_count)
+            waits.append(remote(mine, mine, send_sem.at[at], recv_sem.at[at], section, my_row))
+        return buf, send_sem, recv_sem, across, waits
+
+    def wait_plane(gather):
+        buf, send_sem, recv_sem, across, waits = gather
+        for dr in range(1, row_count):
+            across[dr - 1].wait_recv()
+            row = lax.rem(my_row + row_count - dr, row_count)
+            piece = buf.at[rows_of(my_section * row_count + row)]
+            for ds in range(1, section_count):
+                at = ds * row_count + dr
+                section = lax.rem(my_section + ds, section_count)
+                waits.append(
+                    remote(piece, piece, send_sem.at[at], recv_sem.at[at], section, my_row)
+                )
+        for copy in waits:
             copy.wait_recv()
 
     finals = []
@@ -225,8 +276,8 @@
             piece = dst.at[slot]
             pltpu.make_async_copy(piece, piece, recv_sem.at[slot]).wait()
 
-    first = scatter_plane(part, pr, rs_send, rs_recv)
-    pooled = sum_plane(first, part, pr).astype(jnp.bfloat16)
+    first = relay_plane(scatter_plane(part, pr, pair.at[L], rs_send, rs_recv))
+    pooled = sum_plane(first).astype(jnp.bfloat16)
     xa[0, my_rows, :] = pooled
     gathers = gather_plane(xa.at[0], ag_send.at[0], ag_recv.at[0])
     pooled_wide = pooled.astype(jnp.float32)
@@ -265,23 +316,26 @@
                 preferred_element_type=jnp.float32,
             ).astype(jnp.bfloat16)
 
-        sums = scatter_plane(gpart.at[back], gr.at[back], g_send.at[back], g_recv.at[back])
+        sums = scatter_plane(
+            gpart.at[back], gr.at[back], pair.at[back], g_send.at[back], g_recv.at[back]
+        )
         xa_out[step] = xa[step]
         db_out[back] = db[back]
+        sums = relay_plane(sums)
         wait_rows(mr.at[step], m_recv.at[step])
         for h in range(r):
             value = mr[step, h * C].astype(jnp.float32)
             for col_at in range(1, C):
                 value = value + mr[step, h * C + col_at].astype(jnp.float32)
             mixed[step, :, h * OW : (h + 1) * OW] = value
-        mixed[step] = mixed[step] + bias[step : step + 1, :]
+        mixed[step] = mixed[step] + bias[step : step + 1, pl.ds(pl.multiple_of(c * IW, IW), IW)]
         current = (pooled_wide * mixed[step] + current.astype(jnp.float32)).astype(jnp.bfloat16)
         if step + 1 < L:
             xa[step + 1, my_rows, :] = current
             gathers = gather_plane(xa.at[step + 1], ag_send.at[step + 1], ag_recv.at[step + 1])
         else:
             crossed_out[...] = current
-        kept[back] = kept[back + 1] + sum_plane(sums, gpart.at[back], gr.at[back])
+        kept[back] = kept[back + 1] + sum_plane(sums)
         if back > 0:
             drow[back - 1] = (pooled_wide * kept[back]).astype(jnp.bfloat16)
             send_to_features(
@@ -294,18 +348,48 @@
     pgrad_out[...] = pooled_grad
     ga[my_rows, :] = pooled_grad.astype(jnp.bfloat16)
     gathers = gather_plane(ga, ag_send.at[L], ag_recv.at[L])
-    for copy in sent[: -(N - 1)]:
+    wait_plane(gathers)
+    ga_out[...] = ga[...]
+    for copy in sent:
         copy.wait_send()
-    for remote, copy in finals:
-
-        @pl.when(remote)
+    for sent_off, copy in finals:
+
+        @pl.when(sent_off)
         def _(copy=copy):
             copy.wait_send()
 
-    wait_plane(gathers)
-    ga_out[...] = ga[...]
-    for copy in sent[-(N - 1) :]:
-        copy.wait_send()
+
+def weight_kernel(xa, db, weight_grad, bias_grad):
+    weight_grad[0] = lax.dot_general(
+        xa[0], db[0], (((0,), (0,)), ((), ())), preferred_element_type=jnp.float32
+    )
+
+    @pl.when(pl.program_id(1) == 0)
+    def _():
+        bias_grad[0] = jnp.sum(db[0].astype(jnp.float32), axis=0, keepdims=True)
+
+
+def weight_grads(xa, db):
+    layers, batch_rows, in_width = xa.shape
+    out_width = db.shape[2]
+    tile = math.gcd(in_width, 512)
+    weight_grad, bias_grad = pl.pallas_call(
+        weight_kernel,
+        grid=(layers, in_width // tile),
+        out_shape=(
+            jax.ShapeDtypeStruct((layers, in_width, out_width), jnp.float32),
+            jax.ShapeDtypeStruct((layers, 1, out_width), jnp.float32),
+        ),
+        in_specs=[
+            pl.BlockSpec((1, batch_rows, tile), lambda l, i: (l, 0, i)),
+            pl.BlockSpec((1, batch_rows, out_width), lambda l, i: (l, 0, 0)),
+        ],
+        out_specs=(
+            pl.BlockSpec((1, tile, out_width), lambda l, i: (l, i, 0)),
+            pl.BlockSpec((1, 1, out_width), lambda l, i: (l, 0, 0)),
+        ),
+    )(xa, db)
+    return weight_grad, bias_grad.reshape(layers, out_width)
 
 
 def body(tables, bag_index, cross_weight, cross_bias, upstream):
@@ -317,18 +401,14 @@
     np_count = sizes[0] * sizes[1]
     col_count = sizes[2]
     ratio = in_width // out_width
-    my_row = lax.axis_index(("section", "row"))
-    local_ids = bag_index - my_row * shard_rows
-    counts = jnp.stack(
-        [bag_counts(local_ids[:, feature_at, :], shard_rows) for feature_at in range(feat_count)]
-    )
-    bias = lax.dynamic_slice_in_dim(cross_bias, lax.axis_index("col") * in_width, in_width, axis=1)
+    ids = jnp.transpose(bag_index, (1, 2, 0))
     bf16, f32 = jnp.bfloat16, jnp.float32
     vmem = pl.BlockSpec(memory_space=pltpu.VMEM)
     dma = pltpu.SemaphoreType.DMA
-    xa, db, crossed, pooled_grad, full_grad = pl.pallas_call(
+    counts, xa, db, crossed, pooled_grad, full_grad = pl.pallas_call(
         functools.partial(kernel, sizes),
         out_shape=(
+            jax.ShapeDtypeStruct((feat_count, shard_rows, batch_rows), bf16),
             jax.ShapeDtypeStruct((layers, batch_rows, in_width), bf16),
             jax.ShapeDtypeStruct((layers, batch_rows, out_width), bf16),
             jax.ShapeDtypeStruct((block_rows, in_width), bf16),
@@ -336,11 +416,12 @@
             jax.ShapeDtypeStruct((batch_rows, in_width), bf16),
         ),
         in_specs=[vmem, vmem, vmem, vmem, pl.BlockSpec(memory_space=pl.ANY)],
-        out_specs=(vmem,) * 5,
+        out_specs=(vmem,) * 6,
         scratch_shapes=[
             pltpu.VMEM((layers, in_width, out_width), bf16),
             pltpu.VMEM((batch_rows, in_width), bf16),
             pltpu.VMEM((np_count, block_rows, in_width), bf16),
+            pltpu.VMEM((layers + 1, sizes[1], block_rows, in_width), bf16),
             pltpu.VMEM((layers, batch_rows, in_width), bf16),
             pltpu.VMEM((layers, batch_rows, out_width), bf16),
             pltpu.VMEM((batch_rows, in_width), bf16),
@@ -365,11 +446,10 @@
         compiler_params=pltpu.CompilerParams(
             collective_id=0, has_side_effects=True, vmem_limit_bytes=56 * 1024 * 1024
         ),
-    )(counts, tables, upstream, bias, cross_weight)
-    weight_grad = jnp.einsum("lbi,lbo->lio", xa, db, preferred_element_type=f32)
-    bias_grad = jnp.sum(db, axis=1, dtype=f32)
+    )(ids, tables, upstream, cross_bias, cross_weight)
+    weight_grad, bias_grad = weight_grads(xa, db)
     grad_rows_full = full_grad.reshape(batch_rows, feat_count, entry_width)
-    table_grad = jnp.einsum("fbv,bfe->fve", counts, grad_rows_full, preferred_element_type=f32)
+    table_grad = jnp.einsum("fvb,bfe->fve", counts, grad_rows_full, preferred_element_type=f32)
     return crossed, pooled_grad, table_grad, weight_grad, bias_grad
 
 

time: 102 us -> 77.9 us (0.76)
  other arithmetic: 9.04 us -> 0 us
  matrix products: 11.3 us -> 2.38 us
  Pallas kernels: 74.8 us -> 70.1 us
    pallas_call x1, Pallas kernels: 74.8 us -> 60.6 us  [body(): pl.pallas_call(functools.partial(kernel, sizes), out_shape=(jax.ShapeDtyp...]
    pallas_call x0 -> x1, Pallas kernels: none -> 9.51 us  [weight_grads(): pl.pallas_call(weight_kernel, grid=(layers, in_width // tile), out_shape=...]
    dot_general x2 -> x1, matrix products: 11.3 us -> 2.38 us  [body(): jnp.einsum('fvb,bfe->fve', counts, grad_rows_full, preferred_element_type...]
    reduce_sum x33 -> x0, other arithmetic: 7.88 us -> none  [the longest x32 7.18 us: bag_counts(): summed = summed + jnp.sum(matches, axis=1, dtype=jnp.float32)]
    slice x36 -> x0, local copies, waits for them, and re-layouts: 3.28 us -> none  [bag_counts(): matches = local_ids[:, offset:offset + group_size, None] == slot_ids]
    unnamed x16 -> x3, local copies, waits for them, and re-layouts: 1.34 us -> 4.34 us
where the time goes in v2:
time: 77.9 us; the launch traced here: 77.5 us
  Pallas kernels  70.1 us (90%)
  local copies, waits for them, and re-layouts  4.34 us (6%)
  matrix products  2.38 us (3%)
    pallas_call x1, Pallas kernels, body(): pl.pallas_call(functools.partial(kernel, sizes), out_shape=(jax.ShapeDtyp...  60.6 us
    pallas_call x1, Pallas kernels, weight_grads(): pl.pallas_call(weight_kernel, grid=(layers, in_width // tile), out_shape=...  9.51 us
    unnamed x3, local copies, waits for them, and re-layouts  4.34 us
    dot_general x1, matrix products, body(): jnp.einsum('fvb,bfe->fve', counts, grad_rows_full, preferred_element_type...  2.38 us

profile of v2, /device:TPU:1, one launch (start us, length us, event | category | flops | bytes accessed | tf_op | source)
XLA Modules:
  0.0 77.5 jit_solution(17031553269269197031)
XLA Ops:
  0.6 60.6 %shard_map.92 = (bf16[8,128,128]{2,1,0:T(8,128)(2,1)}, bf16[2,128,2048]{2,1,0:T(8,128)(2,1)}, bf16[2,128,1024]{2,1,0:T(8,128)(2,1)}, bf16[16,2048]{1,0:T(8,128)(...) custom-call(s32[8,32,128]{2,1,0:T(8,128)} %bitcast.10, bf16[8,128,256]{2,1,0:T(8,128)(2,1)} %tables.1, ...), custom_call_target="tpu_custom_call" | custom-call | tf_op jit(solution)/shard_map/pallas_call | solution.py:408
  61.2 9.5 %shard_map.93 = (f32[2,2048,1024]{2,1,0:T(8,128)}, f32[2,1,1024]{2,1,0:T(1,128)}) custom-call(bf16[2,128,2048]{2,1,0:T(8,128)(2,1)} %get-tuple-element.17.xa, bf16[2,128,1024]{2,1,0:T(8,128)(2,1)} %get-tuple-element.18.db), custom_call_target="tpu_custom_call" | custom-call | tf_op jit(solution)/shard_map/pallas_call | solution.py:376
  70.8 1.3 %copy.18 = f32[2,1,1024]{2,0,1:T(2,128)} copy(f32[2,1,1024]{2,1,0:T(1,128)} %get-tuple-element.20) | data formatting | bytes 16384
  72.0 2.4 %fusion = f32[8,128,256]{2,1,0:T(8,128)} fusion(bf16[8,128,128]{2,1,0:T(8,128)(2,1)} %get-tuple-element.15, bf16[16,8,8,256]{3,2,1,0:T(8,128)(2,1)} %bitcast.9), kind=kOutput, calls=%fused_computation | convolution fusion | flops 67108864 | bytes 1835008 | tf_op jit(solution)/shard_map/fvb,bfe->fve/dot_general | solution.py:452
  74.4 1.5 %copy.21 = bf16[16,2048]{1,0:T(8,128)(2,1)} copy(bf16[16,2048]{1,0:T(8,128)(2,1)} %get-tuple-element.26) | data formatting | bytes 131072
  75.9 1.6 %copy.22 = f32[16,2048]{1,0:T(8,128)} copy(f32[16,2048]{1,0:T(8,128)} %get-tuple-element.27) | data formatting | bytes 262144

commit v3 on v2

--- a/solution.py
+++ b/solution.py
@@ -29,6 +29,7 @@
     pgrad_out,
     ga_out,
     w,
+    kept_counts,
     part,
     pr,
     pair,
@@ -42,6 +43,7 @@
     gr,
     mixed,
     w_sem,
+    out_sem,
     rs_send,
     rs_recv,
     ag_send,
@@ -101,12 +103,20 @@
         for j in range(bag_len):
             hits = hits + jnp.where(ids[f, j : j + 1, :] == slots, 1, 0)
         counts = hits.astype(jnp.float32).astype(jnp.bfloat16)
-        counts_out[f] = counts
+        kept_counts[f] = counts
         cols = pl.ds(pl.multiple_of(f * entry, entry), entry)
         part[:, cols] = lax.dot_general(
             counts, tables[f], (((0,), (0,)), ((), ())), preferred_element_type=jnp.float32
         ).astype(jnp.bfloat16)
 
+    leaving = []
+
+    def leave(src, dst):
+        copy = pltpu.make_async_copy(src, dst, out_sem.at[len(leaving)])
+        copy.start()
+        leaving.append(copy)
+
+    leave(kept_counts, counts_out)
     pl.semaphore_wait(barrier, total - 1)
 
     sent = []
@@ -319,8 +329,8 @@
         sums = scatter_plane(
             gpart.at[back], gr.at[back], pair.at[back], g_send.at[back], g_recv.at[back]
         )
-        xa_out[step] = xa[step]
-        db_out[back] = db[back]
+        leave(xa.at[step], xa_out.at[step])
+        leave(db.at[back], db_out.at[back])
         sums = relay_plane(sums)
         wait_rows(mr.at[step], m_recv.at[step])
         for h in range(r):
@@ -349,7 +359,9 @@
     ga[my_rows, :] = pooled_grad.astype(jnp.bfloat16)
     gathers = gather_plane(ga, ag_send.at[L], ag_recv.at[L])
     wait_plane(gathers)
-    ga_out[...] = ga[...]
+    leave(ga, ga_out)
+    for copy in leaving:
+        copy.wait()
     for copy in sent:
         copy.wait_send()
     for sent_off, copy in finals:
@@ -359,37 +371,104 @@
             copy.wait_send()
 
 
-def weight_kernel(xa, db, weight_grad, bias_grad):
-    weight_grad[0] = lax.dot_general(
-        xa[0], db[0], (((0,), (0,)), ((), ())), preferred_element_type=jnp.float32
+def output_kernel(
+    xa_hbm,
+    db_hbm,
+    counts_hbm,
+    ga_hbm,
+    crossed_hbm,
+    pgrad_hbm,
+    weight_grad,
+    bias_grad,
+    table_grad,
+    crossed_out,
+    pgrad_out,
+    xa,
+    db,
+    counts,
+    ga,
+    held,
+    load_sem,
+    sem,
+):
+    pairs = (
+        (xa_hbm, xa),
+        (db_hbm, db),
+        (counts_hbm, counts),
+        (ga_hbm, ga),
+        (crossed_hbm, crossed_out),
+        (pgrad_hbm, pgrad_out),
     )
-
-    @pl.when(pl.program_id(1) == 0)
-    def _():
-        bias_grad[0] = jnp.sum(db[0].astype(jnp.float32), axis=0, keepdims=True)
-
-
-def weight_grads(xa, db):
-    layers, batch_rows, in_width = xa.shape
+    loads = [
+        pltpu.make_async_copy(src, dst, load_sem.at[k]) for k, (src, dst) in enumerate(pairs)
+    ]
+    for load in loads:
+        load.start()
+    loads[0].wait()
+    loads[1].wait()
+    layers, in_width, _ = held.shape
+    tile = math.gcd(in_width, 512)
+    tiles = in_width // tile
+    copies = []
+    for layer in range(layers):
+        for at in range(tiles):
+            rows = slice(at * tile, (at + 1) * tile)
+            held[layer, rows, :] = lax.dot_general(
+                xa[layer, :, rows],
+                db[layer],
+                (((0,), (0,)), ((), ())),
+                preferred_element_type=jnp.float32,
+            )
+            copy = pltpu.make_async_copy(
+                held.at[layer, rows], weight_grad.at[layer, rows], sem.at[layer * tiles + at]
+            )
+            copy.start()
+            copies.append(copy)
+    feats, _, entry = table_grad.shape
+    for load in loads[2:]:
+        load.wait()
+    for f in range(feats):
+        table_grad[f] = jnp.dot(
+            counts[f], ga[:, f * entry : (f + 1) * entry], preferred_element_type=jnp.float32
+        )
+    for layer in range(layers):
+        bias_grad[layer : layer + 1, :] = jnp.sum(
+            db[layer].astype(jnp.float32), axis=0, keepdims=True
+        )
+    for copy in copies:
+        copy.wait()
+
+
+def write_outputs(xa, db, counts, ga, crossed, pgrad):
+    layers, _, in_width = xa.shape
     out_width = db.shape[2]
-    tile = math.gcd(in_width, 512)
-    weight_grad, bias_grad = pl.pallas_call(
-        weight_kernel,
-        grid=(layers, in_width // tile),
+    feats, shard_rows, _ = counts.shape
+    entry = in_width // feats
+    tiles = in_width // math.gcd(in_width, 512)
+    f32 = jnp.float32
+    vmem = pl.BlockSpec(memory_space=pltpu.VMEM)
+    return pl.pallas_call(
+        output_kernel,
         out_shape=(
-            jax.ShapeDtypeStruct((layers, in_width, out_width), jnp.float32),
-            jax.ShapeDtypeStruct((layers, 1, out_width), jnp.float32),
+            jax.ShapeDtypeStruct((layers, in_width, out_width), f32),
+            jax.ShapeDtypeStruct((layers, out_width), f32),
+            jax.ShapeDtypeStruct((feats, shard_rows, entry), f32),
+            jax.ShapeDtypeStruct(crossed.shape, crossed.dtype),
+            jax.ShapeDtypeStruct(pgrad.shape, f32),
         ),
-        in_specs=[
-            pl.BlockSpec((1, batch_rows, tile), lambda l, i: (l, 0, i)),
-            pl.BlockSpec((1, batch_rows, out_width), lambda l, i: (l, 0, 0)),
+        in_specs=[pl.BlockSpec(memory_space=pl.ANY)] * 6,
+        out_specs=(pl.BlockSpec(memory_space=pl.ANY), vmem, vmem, vmem, vmem),
+        scratch_shapes=[
+            pltpu.VMEM(xa.shape, xa.dtype),
+            pltpu.VMEM(db.shape, db.dtype),
+            pltpu.VMEM(counts.shape, counts.dtype),
+            pltpu.VMEM(ga.shape, ga.dtype),
+            pltpu.VMEM((layers, in_width, out_width), f32),
+            pltpu.SemaphoreType.DMA((6,)),
+            pltpu.SemaphoreType.DMA((layers * tiles,)),
         ],
-        out_specs=(
-            pl.BlockSpec((1, tile, out_width), lambda l, i: (l, i, 0)),
-            pl.BlockSpec((1, 1, out_width), lambda l, i: (l, 0, 0)),
-        ),
-    )(xa, db)
-    return weight_grad, bias_grad.reshape(layers, out_width)
+        compiler_params=pltpu.CompilerParams(vmem_limit_bytes=56 * 1024 * 1024),
+    )(xa, db, counts, ga, crossed, pgrad)
 
 
 def body(tables, bag_index, cross_weight, cross_bias, upstream):
@@ -404,6 +483,7 @@
     ids = jnp.transpose(bag_index, (1, 2, 0))
     bf16, f32 = jnp.bfloat16, jnp.float32
     vmem = pl.BlockSpec(memory_space=pltpu.VMEM)
+    hbm = pl.BlockSpec(memory_space=pl.ANY)
     dma = pltpu.SemaphoreType.DMA
     counts, xa, db, crossed, pooled_grad, full_grad = pl.pallas_call(
         functools.partial(kernel, sizes),
@@ -416,9 +496,10 @@
             jax.ShapeDtypeStruct((batch_rows, in_width), bf16),
         ),
         in_specs=[vmem, vmem, vmem, vmem, pl.BlockSpec(memory_space=pl.ANY)],
-        out_specs=(vmem,) * 6,
+        out_specs=(hbm, hbm, hbm, vmem, vmem, hbm),
         scratch_shapes=[
             pltpu.VMEM((layers, in_width, out_width), bf16),
+            pltpu.VMEM((feat_count, shard_rows, batch_rows), bf16),
             pltpu.VMEM((batch_rows, in_width), bf16),
             pltpu.VMEM((np_count, block_rows, in_width), bf16),
             pltpu.VMEM((layers + 1, sizes[1], block_rows, in_width), bf16),
@@ -432,6 +513,7 @@
             pltpu.VMEM((layers, np_count, block_rows, in_width), bf16),
             pltpu.VMEM((layers, block_rows, in_width), f32),
             dma((layers,)),
+            dma((2 * layers + 2,)),
             dma((np_count,)),
             dma((np_count,)),
             dma((layers + 1, np_count)),
@@ -447,9 +529,9 @@
             collective_id=0, has_side_effects=True, vmem_limit_bytes=56 * 1024 * 1024
         ),
     )(ids, tables, upstream, cross_bias, cross_weight)
-    weight_grad, bias_grad = weight_grads(xa, db)
-    grad_rows_full = full_grad.reshape(batch_rows, feat_count, entry_width)
-    table_grad = jnp.einsum("fvb,bfe->fve", counts, grad_rows_full, preferred_element_type=f32)
+    weight_grad, bias_grad, table_grad, crossed, pooled_grad = write_outputs(
+        xa, db, counts, full_grad, crossed, pooled_grad
+    )
     return crossed, pooled_grad, table_grad, weight_grad, bias_grad
 
 

time: 77.9 us -> 70.4 us (0.904)
  local copies, waits for them, and re-layouts: 4.34 us -> 0 us
  matrix products: 2.38 us -> 0 us
    unnamed x3 -> x0, local copies, waits for them, and re-layouts: 4.34 us -> none
    dot_general x1 -> x0, matrix products: 2.38 us -> none  [body(): jnp.einsum('fvb,bfe->fve', counts, grad_rows_full, preferred_element_type...]
where the time goes in v3:
time: 70.4 us; the launch traced here: 70.3 us
  Pallas kernels  69.6 us (99%)
    pallas_call x1, Pallas kernels, body(): pl.pallas_call(functools.partial(kernel, sizes), out_shape=(jax.ShapeDtyp...  60.8 us
    pallas_call x1, Pallas kernels, write_outputs(): pl.pallas_call(output_kernel, out_shape=(jax.ShapeDtypeStruct((layers, in...  8.82 us

profile of v3, /device:TPU:1, one launch (start us, length us, event | category | flops | bytes accessed | tf_op | source)
XLA Modules:
  0.0 70.3 jit_solution(7931624097634813537)
XLA Ops:
  0.6 60.8 %shard_map.92 = (bf16[8,128,128]{2,1,0:T(8,128)(2,1)}, bf16[2,128,2048]{2,1,0:T(8,128)(2,1)}, bf16[2,128,1024]{2,1,0:T(8,128)(2,1)}, bf16[16,2048]{1,0:T(8,128)(...) custom-call(s32[8,32,128]{2,1,0:T(8,128)} %bitcast.1, bf16[8,128,256]{2,1,0:T(8,128)(2,1)} %tables.1, ...), custom_call_target="tpu_custom_call" | custom-call | tf_op jit(solution)/shard_map/pallas_call | solution.py:488
  61.4 8.8 %shard_map.93 = (f32[2,2048,1024]{2,1,0:T(8,128)}, f32[2,1024]{1,0:T(2,128)}, f32[8,128,256]{2,1,0:T(8,128)}, bf16[16,2048]{1,0:T(8,128)(2,1)}, f32[16,2048]{1,0:T(8,128)}) custom-call(bf16[2,128,2048]{2,1,0:T(8,128)(2,1)} %get-tuple-element.16.xa_hbm, bf16[2,128,1024]{2,1,0:T(8,128)(2,1)} %get-tuple-element.17.db_hbm, ...), custom_call_target="tpu_custom_call" | custom-call | tf_op jit(solution)/shard_map/pallas_call | solution.py:450

commit v4 on v3

--- a/solution.py
+++ b/solution.py
@@ -391,9 +391,10 @@
     load_sem,
     sem,
 ):
+    layers, in_width, _ = held.shape
     pairs = (
-        (xa_hbm, xa),
-        (db_hbm, db),
+        *((xa_hbm.at[layer], xa.at[layer]) for layer in range(layers)),
+        *((db_hbm.at[layer], db.at[layer]) for layer in range(layers)),
         (counts_hbm, counts),
         (ga_hbm, ga),
         (crossed_hbm, crossed_out),
@@ -404,13 +405,12 @@
     ]
     for load in loads:
         load.start()
-    loads[0].wait()
-    loads[1].wait()
-    layers, in_width, _ = held.shape
-    tile = math.gcd(in_width, 512)
+    tile = math.gcd(in_width, 256)
     tiles = in_width // tile
     copies = []
     for layer in range(layers):
+        loads[layer].wait()
+        loads[layers + layer].wait()
         for at in range(tiles):
             rows = slice(at * tile, (at + 1) * tile)
             held[layer, rows, :] = lax.dot_general(
@@ -425,7 +425,7 @@
             copy.start()
             copies.append(copy)
     feats, _, entry = table_grad.shape
-    for load in loads[2:]:
+    for load in loads[2 * layers :]:
         load.wait()
     for f in range(feats):
         table_grad[f] = jnp.dot(
@@ -444,7 +444,7 @@
     out_width = db.shape[2]
     feats, shard_rows, _ = counts.shape
     entry = in_width // feats
-    tiles = in_width // math.gcd(in_width, 512)
+    tiles = in_width // math.gcd(in_width, 256)
     f32 = jnp.float32
     vmem = pl.BlockSpec(memory_space=pltpu.VMEM)
     return pl.pallas_call(
@@ -464,7 +464,7 @@
             pltpu.VMEM(counts.shape, counts.dtype),
             pltpu.VMEM(ga.shape, ga.dtype),
             pltpu.VMEM((layers, in_width, out_width), f32),
-            pltpu.SemaphoreType.DMA((6,)),
+            pltpu.SemaphoreType.DMA((2 * layers + 4,)),
             pltpu.SemaphoreType.DMA((layers * tiles,)),
         ],
         compiler_params=pltpu.CompilerParams(vmem_limit_bytes=56 * 1024 * 1024),

time: 70.4 us -> 70.2 us (level)
  no operation moved by 1% of the time
where the time goes in v4:
time: 70.2 us; the launch traced here: 70.1 us
  Pallas kernels  69.4 us (99%)
    pallas_call x1, Pallas kernels, body(): pl.pallas_call(functools.partial(kernel, sizes), out_shape=(jax.ShapeDtyp...  60.8 us
    pallas_call x1, Pallas kernels, write_outputs(): pl.pallas_call(output_kernel, out_shape=(jax.ShapeDtypeStruct((layers, in...  8.65 us

profile of v4, /device:TPU:1, one launch (start us, length us, event | category | flops | bytes accessed | tf_op | source)
XLA Modules:
  0.0 70.1 jit_solution(14784021210218864987)
XLA Ops:
  0.6 60.8 %shard_map.92 = (bf16[8,128,128]{2,1,0:T(8,128)(2,1)}, bf16[2,128,2048]{2,1,0:T(8,128)(2,1)}, bf16[2,128,1024]{2,1,0:T(8,128)(2,1)}, bf16[16,2048]{1,0:T(8,128)(...) custom-call(s32[8,32,128]{2,1,0:T(8,128)} %bitcast.1, bf16[8,128,256]{2,1,0:T(8,128)(2,1)} %tables.1, ...), custom_call_target="tpu_custom_call" | custom-call | tf_op jit(solution)/shard_map/pallas_call | solution.py:488
  61.4 8.6 %shard_map.93 = (f32[2,2048,1024]{2,1,0:T(8,128)}, f32[2,1024]{1,0:T(2,128)}, f32[8,128,256]{2,1,0:T(8,128)}, bf16[16,2048]{1,0:T(8,128)(2,1)}, f32[16,2048]{1,0:T(8,128)}) custom-call(bf16[2,128,2048]{2,1,0:T(8,128)(2,1)} %get-tuple-element.16.xa_hbm, bf16[2,128,1024]{2,1,0:T(8,128)(2,1)} %get-tuple-element.17.db_hbm, ...), custom_call_target="tpu_custom_call" | custom-call | tf_op jit(solution)/shard_map/pallas_call | solution.py:450
